TPU v7x, 256 devices: a whole 4x4x8 slice. The times are simulated.
256 devices in a mesh: tm: 8 (over z_hi, y), gy: 4 (over z_lo), gz: 8 (over x, core).
Axes of the slice: x: 4, y: 4, z: 8 (z_hi: 2, z_lo: 4; z = z_hi * 4 + z_lo), core: 2. Of those that a mesh axis runs over, the one named last changes fastest.
Arguments:
- inverse_mass: float32 [32, 128, 128], P('gy', 'gz'), may hold values from 0.5 to 2
- actuator_of_cell: int32 [32, 128, 128], P('gy', 'gz'), may hold values from 0 to 31
- plan_ids: int32 [8, 32], P('tm'), may hold values from 0 to 15
- profiles: float32 [16, 9], replicated, may hold values from -4 to 4
- directions: float32 [3, 32], replicated, may hold values from -4 to 4
Outputs:
- predicted_state: float32 [8, 6, 32, 128, 128], P('tm', None, 'gy', 'gz')
All inputs are finite; a program needn't handle non-finite values.
Results may differ from a plain program's by a relative error of at most 0.00021.
Values sent between devices are 32-bit elements; how exact they have to be, the bound alone decides.
No kernel may reach another device: no remote copies, remote signals or barrier semaphores. Data moves between devices by JAX's collectives and lax.ppermute only.
A program may use at most 64 MiB of HBM per device.

v0:
```python
import functools
import math

import jax
import jax.numpy as jnp
import numpy as np
from jax import lax
from jax.experimental import pallas as pl
from jax.experimental.pallas import tpu as pltpu
from jax.sharding import PartitionSpec as P

STEPS = 8
TERMS = 8
lame_ratio = 2.5
mass_top = 2.0
step_squared = 1.0

PLANES = 32
OWN_Y = 8
OWN_Z = 16
HALO = 24
ROWS = HALO + OWN_Z + HALO
PAD = 8
LANES = 128
CHUNK = 8
UNROLL = 2


def cheb_tables():
    spectrum_top = mass_top * 12.0 * (1.0 + lame_ratio)
    time_step = math.sqrt(step_squared / spectrum_top)
    horizon = STEPS * time_step
    angles = np.pi * (np.arange(TERMS) + 0.5) / TERMS
    node_x = 0.5 * spectrum_top * (1.0 + np.cos(angles))
    node_root = np.sqrt(node_x)
    values_c = np.cos(horizon * node_root)
    values_s = np.sin(horizon * node_root) / node_root
    values_g = node_root * np.sin(horizon * node_root)

    def project_values(values):
        result = np.array([2.0 / TERMS * np.sum(values * np.cos(k * angles)) for k in range(TERMS)])
        result[0] = 0.5 * result[0]
        return [float(entry) for entry in result]

    return (
        spectrum_top,
        time_step,
        project_values(values_c),
        project_values(values_s),
        project_values(values_g),
    )


def columns(reach):
    return (HALO - reach) // 8, -(-(HALO + OWN_Z + reach) // 8)


def span(reach):
    count = min(8, reach) + OWN_Y + min(16, reach)
    return count + count % UNROLL


def kernel(
    place_ref, table_ref, far_left, left, own, right, far_right, out_ref,
    mass, mass4, diag, diag_x, actor, dirs, disp, vel, spare_u, spare_v, total, div_u, div_v,
):
    spectrum_top, time_step, coef_c, coef_s, coef_g = cheb_tables()
    here = place_ref[0]
    home = here * OWN_Y
    lane = lax.broadcasted_iota(jnp.int32, (CHUNK, LANES), 1)
    not_first = lane != 0
    not_last = lane != LANES - 1
    six_x = jnp.where(lane == 0, 6.0 + lame_ratio, 6.0).astype(jnp.float32)
    zero = jnp.zeros((CHUNK, LANES), jnp.float32)

    def after(value):
        return jnp.where(not_last, pltpu.roll(value, LANES - 1, 1), 0.0)

    def before(value):
        return jnp.where(not_first, pltpu.roll(value, 1, 1), 0.0)

    def rows_of(column):
        return PAD + column * 8

    def lowest(reach):
        return jnp.clip(home - reach, 0, PLANES - span(reach)) + 1

    def zero_array(ref, lead):
        @pl.loop(0, ref.shape[-3])
        def _(plane):
            for c in lead:
                ref[c + (plane,)] = jnp.zeros(ref.shape[-2:], ref.dtype)

    three = [(0,), (1,), (2,)]
    for ref in (disp, vel, spare_u, spare_v):
        zero_array(ref, three)

    for ref in (mass, mass4, diag, diag_x, div_u, div_v):
        zero_array(ref, [()])

    for slot in range(4):
        first = lax.rem(here + 4 - slot, 4) * OWN_Y + 1

        @pl.loop(0, OWN_Y)
        def _(y):
            plane = first + y
            row = 0
            for piece in (far_left, left, own, right, far_right):
                for part in range(0, piece.shape[-2], 8):
                    at = pl.ds(PAD + row, 8)
                    weight = piece[slot, 0, y, part : part + 8, :] * (1.0 / spectrum_top)
                    index = piece[slot, 1, y, part : part + 8, :].astype(jnp.int32)
                    mass[plane, at, :] = weight
                    mass4[plane, at, :] = 4.0 * weight
                    diag[plane, at, :] = 24.0 * weight - 2.0
                    diag_x[plane, at, :] = 4.0 * six_x * weight - 2.0
                    actor[plane, at, :] = index
                    for c in range(3):
                        dirs[c, plane, at, :] = jnp.take_along_axis(
                            table_ref[27 + c], index, axis=1, mode="promise_in_bounds"
                        )
                    row += 8

    def divergence(field, plane, at, low):
        a0, a1, a2 = (field[c, plane, at, :] for c in range(3))
        nxt = after(a2)
        value = (field[0, plane + 1, at, :] - a0) + (field[1, plane, pl.ds(low + 1, CHUNK), :] - a1)
        return (value + (nxt - a2)) * lame_ratio, nxt

    def parts(field, div, plane, low):
        at = pl.ds(low, CHUNK)
        u0, u1, u2 = (field[c, plane, at, :] for c in range(3))
        up = [field[c, plane + 1, at, :] for c in range(3)]
        down = [field[c, plane - 1, at, :] for c in range(3)]
        ahead = [field[c, plane, pl.ds(low + 1, CHUNK), :] for c in range(3)]
        behind = [field[c, plane, pl.ds(low - 1, CHUNK), :] for c in range(3)]
        next2 = after(u2)
        here_p = ((up[0] - u0) + (ahead[1] - u1) + (next2 - u2)) * lame_ratio
        div[plane, at, :] = here_p
        side = [(up[c] + down[c]) + (ahead[c] + behind[c]) for c in range(3)]
        sum0 = side[0] + (after(u0) + before(u0)) + (here_p - div[plane - 1, at, :])
        sum1 = side[1] + (after(u1) + before(u1)) + (here_p - div[plane, pl.ds(low - 1, CHUNK), :])
        sum2 = side[2] + (next2 + here_p) - before(here_p - u2)
        return (u0, u1, u2), (sum0, sum1, sum2)

    def sweep(reach, fields, head, each):
        j0, j1 = columns(reach)
        j0p = j0 - 1 if (HALO - reach) % 8 == 0 else j0
        begin = lowest(reach)

        def edges(plane, cols):
            for low in range(rows_of(cols[0]), rows_of(cols[1]), CHUNK):
                at = pl.ds(low, CHUNK)
                for field, div in fields:
                    div[plane, at, :] = divergence(field, plane, at, low)[0]

        if head is not None:
            head(begin - 1)
            head(begin)
        edges(begin - 1, (j0, j1))

        @pl.loop(0, span(reach) // UNROLL)
        def _(trip):
            for q in range(UNROLL):
                plane = begin + trip * UNROLL + q
                if head is not None:
                    head(plane + 1)
                if j0p < j0:
                    edges(plane, (j0p, j0))
                for low in range(rows_of(j0), rows_of(j1), CHUNK):
                    each(plane, low)

    def drive(window, reach_last):
        def amplitude(n, plane, at):
            return jnp.take_along_axis(
                table_ref[window * 9 + n], actor[plane, at, :], axis=1, mode="promise_in_bounds"
            )

        reach = reach_last + STEPS
        j0, j1 = columns(reach)

        @pl.loop(0, span(reach))
        def _(y):
            plane = lowest(reach) + y
            for low in range(rows_of(j0), rows_of(j1), CHUNK):
                at = pl.ds(low, CHUNK)
                push = (0.5 * mass[plane, at, :]) * amplitude(0, plane, at)
                for c in range(3):
                    disp[c, plane, at, :] = zero
                    vel[c, plane, at, :] = push * dirs[c, plane, at, :]

        for n in range(STEPS):
            reach = reach_last + STEPS - 1 - n
            j0, j1 = columns(reach + 1)
            last = n == STEPS - 1

            def head(plane):
                for low in range(rows_of(j0), rows_of(j1), CHUNK):
                    at = pl.ds(low, CHUNK)
                    for c in range(3):
                        disp[c, plane, at, :] = disp[c, plane, at, :] + vel[c, plane, at, :]

            def each(plane, low):
                at = pl.ds(low, CHUNK)
                centre, sums = parts(disp, div_u, plane, low)
                amp = amplitude(n + 1, plane, at)
                weight = mass[plane, at, :]
                for c in range(3):
                    six = six_x if c == 2 else 6.0
                    change = weight * ((dirs[c, plane, at, :] * amp + sums[c]) - six * centre[c])
                    if last:
                        vel[c, plane, at, :] = (vel[c, plane, at, :] + 0.5 * change) * (1.0 / time_step)
                    else:
                        vel[c, plane, at, :] = vel[c, plane, at, :] + change

            sweep(reach, [(disp, div_u)], head, each)

    def propagate(reach_last):
        even, odd = (disp, vel), (spare_u, spare_v)
        divs = (div_u, div_v)
        j0, j1 = columns(reach_last)
        begin = lowest(reach_last)

        def gather(k):
            @pl.loop(0, span(reach_last))
            def _(y):
                plane = begin + y
                for low in range(rows_of(j0), rows_of(j1), CHUNK):
                    at = pl.ds(low, CHUNK)
                    for c in range(3):
                        u0, v0 = (ref[c, plane, at, :] for ref in even)
                        u1, v1 = (ref[c, plane, at, :] for ref in odd)
                        new_u = (coef_c[k] * u0 + coef_s[k] * v0) + (
                            coef_c[k + 1] * u1 + coef_s[k + 1] * v1
                        )
                        new_v = (coef_c[k] * v0 - coef_g[k] * u0) + (
                            coef_c[k + 1] * v1 - coef_g[k + 1] * u1
                        )
                        if k:
                            new_u = total[c, plane, at, :] + new_u
                            new_v = total[3 + c, plane, at, :] + new_v
                        total[c, plane, at, :] = new_u
                        total[3 + c, plane, at, :] = new_v

        for k in range(1, TERMS):
            reach = reach_last + TERMS - 1 - k
            source, target = (even, odd) if k % 2 else (odd, even)

            def each(plane, low):
                at = pl.ds(low, CHUNK)
                weight = mass4[plane, at, :]
                middle = diag[plane, at, :]
                middle_x = diag_x[plane, at, :]
                for field, div, result in zip(source, divs, target):
                    centre, sums = parts(field, div, plane, low)
                    for c in range(3):
                        own_part = (middle_x if c == 2 else middle) * centre[c]
                        value = own_part - weight * sums[c]
                        if k == 1:
                            result[c, plane, at, :] = 0.5 * value
                        else:
                            result[c, plane, at, :] = value - result[c, plane, at, :]

            sweep(reach, list(zip(source, divs)), None, each)
            if k % 2:
                gather(k - 1)

    drive(0, 2 * (TERMS - 1))
    propagate(TERMS - 1)
    drive(1, TERMS - 1)
    j0, j1 = columns(TERMS - 1)

    @pl.loop(0, span(TERMS - 1))
    def _(y):
        plane = lowest(TERMS - 1) + y
        for low in range(rows_of(j0), rows_of(j1), CHUNK):
            at = pl.ds(low, CHUNK)
            for c in range(3):
                disp[c, plane, at, :] = disp[c, plane, at, :] + total[c, plane, at, :]
                vel[c, plane, at, :] = vel[c, plane, at, :] + total[3 + c, plane, at, :]

    propagate(0)
    drive(2, 0)

    @pl.loop(0, OWN_Y)
    def _(y):
        plane = home + 1 + y
        at = pl.ds(PAD + HALO, OWN_Z)
        for c in range(3):
            out_ref[c, y, :, :] = disp[c, plane, at, :] + total[c, plane, at, :]
            out_ref[3 + c, y, :, :] = vel[c, plane, at, :] + total[3 + c, plane, at, :]


def predict(place, table, far_left, left, own, right, far_right):
    box = (PLANES + 2, PAD + ROWS + PAD, LANES)
    f32 = jnp.float32
    vmem = pl.BlockSpec(memory_space=pltpu.VMEM)
    return pl.pallas_call(
        kernel,
        out_shape=jax.ShapeDtypeStruct((6, OWN_Y, OWN_Z, LANES), f32),
        in_specs=[pl.BlockSpec(memory_space=pltpu.SMEM)] + [vmem] * 6,
        out_specs=vmem,
        scratch_shapes=[pltpu.VMEM(box, f32)] * 4
        + [pltpu.VMEM(box, jnp.int32), pltpu.VMEM((3,) + box, f32)]
        + [pltpu.VMEM((3,) + box, f32)] * 4
        + [pltpu.VMEM((6,) + box, f32)]
        + [pltpu.VMEM(box, f32)] * 2,
        compiler_params=pltpu.CompilerParams(vmem_limit_bytes=60 * 1024 * 1024),
    )(place, table, far_left, left, own, right, far_right)


def lookup_tables(plan, profiles, directions):
    window = lax.axis_index("tm")
    count = lax.axis_size("tm")
    plans = [
        lax.ppermute(plan, "tm", [(i, i + back) for i in range(count - back)]) for back in (2, 1)
    ] + [plan]
    rows = []
    for back, ids in zip((2, 1, 0), plans):
        picked = ids[0][:, None] == jnp.arange(profiles.shape[0], dtype=jnp.int32)[None, :]
        picked = jnp.where(window >= back, picked, False).astype(jnp.float32)
        chosen = jnp.dot(
            picked, profiles, precision=lax.Precision.HIGHEST, preferred_element_type=jnp.float32
        )
        rows.append(chosen.T)
    table = jnp.concatenate(rows + [directions], axis=0)
    table = jnp.pad(table, ((0, 2), (0, LANES - table.shape[1])))
    return jnp.broadcast_to(table[:, None, :], (32, CHUNK, LANES))


def ring_steps(step):
    pairs = []
    for ring in range(8):
        move = step(ring)
        goal = (ring + move) % 8
        for y in range(4):
            source = ((ring // 4) * 4 + y) * 4 + ring % 4
            target = ((goal // 4) * 4 + y) * 4 + goal % 4
            pairs.append((source, target))
    return pairs


def body(inverse_mass, actuator_of_cell, plan_ids, profiles, directions):
    place = lax.axis_index("gy").astype(jnp.int32)[None]
    packed = jnp.stack([inverse_mass, actuator_of_cell.astype(jnp.float32)])
    table = lookup_tables(plan_ids, profiles, directions)
    from_lower = lax.ppermute(packed, ("tm", "gy"), ring_steps(lambda ring: 1))
    from_upper = lax.ppermute(packed, ("tm", "gy"), ring_steps(lambda ring: 7))
    opposite = lax.ppermute(packed, ("tm", "gy"), ring_steps(lambda ring: 2 if ring % 2 else 6))
    column = jnp.stack([packed, from_lower, opposite, from_upper])
    count = lax.axis_size("gz")

    def shifted(block, step):
        return lax.ppermute(
            block, "gz", [(i, i + step) for i in range(count) if 0 <= i + step < count]
        )

    left = shifted(column, 1)
    right = shifted(column, -1)
    far_left = shifted(column[..., 8:, :], 2)
    far_right = shifted(column[..., :8, :], -2)
    result = predict(place, table, far_left, left, column, right, far_right)
    return result[None]


def solution(mesh):
    in_specs = (P("gy", "gz", None), P("gy", "gz", None), P("tm", None), P(), P())
    out_specs = P("tm", None, "gy", "gz", None)
    return jax.shard_map(body, mesh=mesh, in_specs=in_specs, out_specs=out_specs, check_vma=False)
```

profile of v0, /device:TPU:27, one launch (start us, length us, event | category | flops | bytes accessed | tf_op | source)
XLA Modules:
  0.0 165.9 jit_solution(10538470054745508818)
XLA Ops:
  0.0 0.0 copy-start
  0.0 0.0 copy-start.6
  0.0 9.6 %collective-permute-start = (s32[1,32]{1,0:T(1,128)}, s32[1,32]{1,0:T(1,128)S(1)}, u32[]{:S(2)}, u32[]{:S(2)}) collective-permute-start(s32[1,32]{1,0:T(1,128)} %param.7), channel_id=1, source_target_pairs={{0,64},{32,96},{64,128},{96,160},{128,192},{160,224},{1,65},{33,97... | collective-permute-start | bytes 392 | tf_op jit(solution)/shard_map/ppermute | solution.py:316
  9.6 3.8 %collective-permute-start.1 = (s32[1,32]{1,0:T(1,128)}, s32[1,32]{1,0:T(1,128)S(1)}, u32[]{:S(2)}, u32[]{:S(2)}) collective-permute-start(s32[1,32]{1,0:T(1,128)} %param.7), channel_id=1, source_target_pairs={{0,32},{32,64},{64,96},{96,128},{128,160},{160,192},{192,224},{1,3... | collective-permute-start | bytes 392 | tf_op jit(solution)/shard_map/ppermute | solution.py:316
  13.4 0.8 convert_bitcast_fusion
  14.3 0.0 copy-done.6
  14.3 0.1 collective-permute-start.3
  14.4 1.9 %collective-permute-start.2 = (f32[2,8,16,128]{3,2,1,0:T(8,128)S(1)}, f32[2,8,16,128]{3,2,1,0:T(8,128)S(1)}, u32[]{:S(2)}, u32[]{:S(2)}) collective-permute-start(f32[2,8,16,128]{3,2,1,0:T(8,128)S(1)} %get-tuple-element.8), channel_id=1, source_target_pairs={{0,8},{32,40},{64,72},{96,104},{8,16},{40,48},{72,80},{104,112},{1... | collective-permute-start | bytes 393224 | tf_op jit(solution)/shard_map/ppermute | solution.py:347
  16.3 1.2 collective-permute-start.4
  17.5 0.0 copy-start.8
  17.5 0.0 copy-done
  17.5 0.7 copy-done.8
  18.2 0.2 convolution_bitcast_fusion
  18.4 0.0 collective-permute-done
  18.4 0.2 convolution_bitcast_fusion.2
  18.6 0.5 collective-permute-done.3
  19.1 3.2 %collective-permute-done.2 = f32[2,8,16,128]{3,2,1,0:T(8,128)S(1)} collective-permute-done((f32[2,8,16,128]{3,2,1,0:T(8,128)S(1)}, f32[2,8,16,128]{3,2,1,0:T(8,128)S(1)}, u32[]{:S(2)}, u32[]{:S(2)}) %collective-permute-start.2) | collective-permute-done | bytes 131104 | tf_op jit(solution)/shard_map/ppermute | solution.py:347
  22.4 0.1 collective-permute-done.4
  22.6 0.0 copy-start.1
  22.6 4.2 %collective-permute-start.7 = (f32[4,2,8,16,128]{4,3,2,1,0:T(8,128)S(1)}, f32[4,2,8,16,128]{4,3,2,1,0:T(8,128)S(1)}, u32[]{:S(2)}, u32[]{:S(2)}) collective-permute-start(f32[4,2,8,16,128]{4,3,2,1,0:T(8,128)S(1)} %pad_maximum_fusion.own), channel_id=1, source_target_pairs={{1,0},{2,1},{3,2},{4,3},{5,4},{6,5},{7,6},{9,8},{10,9},{11,10},{12... | collective-permute-start | bytes 1572872 | tf_op jit(solution)/shard_map/ppermute | solution.py:354
  26.8 3.0 %collective-permute-start.6 = (f32[4,2,8,16,128]{4,3,2,1,0:T(8,128)S(1)}, f32[4,2,8,16,128]{4,3,2,1,0:T(8,128)S(1)}, u32[]{:S(2)}, u32[]{:S(2)}) collective-permute-start(f32[4,2,8,16,128]{4,3,2,1,0:T(8,128)S(1)} %pad_maximum_fusion.own), channel_id=1, source_target_pairs={{0,1},{1,2},{2,3},{3,4},{4,5},{5,6},{6,7},{8,9},{9,10},{10,11},{11... | collective-permute-start | bytes 1572872 | tf_op jit(solution)/shard_map/ppermute | solution.py:354
  29.8 0.1 fusion.19
  29.8 0.0 copy-done.1
  29.9 2.2 %collective-permute-start.8 = (f32[4,2,8,8,128]{4,3,2,1,0:T(8,128)S(1)}, f32[4,2,8,8,128]{4,3,2,1,0:T(8,128)S(1)}, u32[]{:S(2)}, u32[]{:S(2)}) collective-permute-start(f32[4,2,8,8,128]{4,3,2,1,0:T(8,128)S(1)} %get-tuple-element.5), channel_id=1, source_target_pairs={{2,0},{3,1},{4,2},{5,3},{6,4},{7,5},{10,8},{11,9},{12,10},{13,11},... | collective-permute-start | bytes 786440 | tf_op jit(solution)/shard_map/ppermute | solution.py:354
  32.0 3.1 %collective-permute-start.5 = (f32[4,2,8,8,128]{4,3,2,1,0:T(8,128)S(1)}, f32[4,2,8,8,128]{4,3,2,1,0:T(8,128)S(1)}, u32[]{:S(2)}, u32[]{:S(2)}) collective-permute-start(f32[4,2,8,8,128]{4,3,2,1,0:T(8,128)S(1)} %get-tuple-element.6), channel_id=1, source_target_pairs={{0,2},{1,3},{2,4},{3,5},{4,6},{5,7},{8,10},{9,11},{10,12},{11,13},... | collective-permute-start | bytes 786440 | tf_op jit(solution)/shard_map/ppermute | solution.py:354
  35.2 0.0 collective-permute-done.1
  35.2 0.0 copy-start.7
  35.2 0.2 convolution_bitcast_fusion.1
  35.4 0.5 copy-done.7
  35.9 4.2 %collective-permute-done.8.far_right = f32[4,2,8,8,128]{4,3,2,1,0:T(8,128)S(1)} collective-permute-done((f32[4,2,8,8,128]{4,3,2,1,0:T(8,128)S(1)}, f32[4,2,8,8,128]{4,3,2,1,0:T(8,128)S(1)}, u32[]{:S(2)}, u32[]{:S(2)}) %collective-permute-start.8) | collective-permute-done | bytes 262176 | tf_op jit(solution)/shard_map/ppermute | solution.py:354
  40.1 0.0 copy-start.4
  40.1 2.3 %collective-permute-done.5.far_left = f32[4,2,8,8,128]{4,3,2,1,0:T(8,128)S(1)} collective-permute-done((f32[4,2,8,8,128]{4,3,2,1,0:T(8,128)S(1)}, f32[4,2,8,8,128]{4,3,2,1,0:T(8,128)S(1)}, u32[]{:S(2)}, u32[]{:S(2)}) %collective-permute-start.5) | collective-permute-done | bytes 262176 | tf_op jit(solution)/shard_map/ppermute | solution.py:354
  42.4 0.0 copy-start.5
  42.4 0.0 collective-permute-done.7.right
  42.4 0.0 copy-start.2
  42.4 0.0 collective-permute-done.6.left
  42.4 0.0 copy-start.3
  42.4 0.7 broadcast_in_dim.23.table_ref
  43.2 0.0 copy-done.4
  43.2 0.0 copy-done.5
  43.2 0.2 copy-done.2
  43.4 0.2 copy-done.3
  43.5 122.4 %shard_map.55 = f32[6,8,16,128]{3,2,1,0:T(8,128)} custom-call(s32[1]{0:T(128)} %bitcast.place_ref, f32[32,8,128]{2,1,0:T(8,128)} %broadcast_in_dim.23.table_ref, f32[4,2,8,8,128]{4,3,2,1,0:T(8,128)} %copy-done.5, f32[4,2,8,16,128]{4,3,2,1,0:T(8,128)} %copy-done.3, f32[4,2,8,16,128]{4,3,2,1,0:T(8,128)} %copy-done.1, f32[4,2,8,16,128]{4,3,2,1,0:T(8,128)} %copy-done.2, ...), custom_call_target="tpu_custom_call" | custom-call | tf_op jit(solution)/shard_map/pallas_call | solution.py:298
  (3 shorter events, 0.1 us)
Async XLA Ops:
  0.0 17.5 %copy-start = (f32[16,9]{1,0:T(8,128)S(1)}, f32[16,9]{1,0:T(8,128)}, u32[]{:S(2)}) copy-start(f32[16,9]{1,0:T(8,128)} %param.8) | copy-start | bytes 1732
  0.0 14.3 %copy-start.6 = (f32[8,16,128]{2,1,0:T(8,128)S(1)}, f32[8,16,128]{2,1,0:T(8,128)}, u32[]{:S(2)}) copy-start(f32[8,16,128]{2,1,0:T(8,128)} %param.5) | copy-start | bytes 196612
  0.0 18.4 %collective-permute-start = (s32[1,32]{1,0:T(1,128)}, s32[1,32]{1,0:T(1,128)S(1)}, u32[]{:S(2)}, u32[]{:S(2)}) collective-permute-start(s32[1,32]{1,0:T(1,128)} %param.7), channel_id=1, source_target_pairs={{0,64},{32,96},{64,128},{96,160},{128,192},{160,224},{1,65},{33,97... | collective-permute-start | bytes 392 | tf_op jit(solution)/shard_map/ppermute | solution.py:316
  9.6 25.5 %collective-permute-start.1 = (s32[1,32]{1,0:T(1,128)}, s32[1,32]{1,0:T(1,128)S(1)}, u32[]{:S(2)}, u32[]{:S(2)}) collective-permute-start(s32[1,32]{1,0:T(1,128)} %param.7), channel_id=1, source_target_pairs={{0,32},{32,64},{64,96},{96,128},{128,160},{160,192},{192,224},{1,3... | collective-permute-start | bytes 392 | tf_op jit(solution)/shard_map/ppermute | solution.py:316
  14.3 4.8 %collective-permute-start.3 = (f32[2,8,16,128]{3,2,1,0:T(8,128)S(1)}, f32[2,8,16,128]{3,2,1,0:T(8,128)S(1)}, u32[]{:S(2)}, u32[]{:S(2)}) collective-permute-start(f32[2,8,16,128]{3,2,1,0:T(8,128)S(1)} %get-tuple-element.8), channel_id=1, source_target_pairs={{0,144},{32,176},{64,208},{96,240},{8,24},{40,56},{72,88},{104,120... | collective-permute-start | bytes 393224 | tf_op jit(solution)/shard_map/ppermute | solution.py:349
  14.4 8.0 %collective-permute-start.2 = (f32[2,8,16,128]{3,2,1,0:T(8,128)S(1)}, f32[2,8,16,128]{3,2,1,0:T(8,128)S(1)}, u32[]{:S(2)}, u32[]{:S(2)}) collective-permute-start(f32[2,8,16,128]{3,2,1,0:T(8,128)S(1)} %get-tuple-element.8), channel_id=1, source_target_pairs={{0,8},{32,40},{64,72},{96,104},{8,16},{40,48},{72,80},{104,112},{1... | collective-permute-start | bytes 393224 | tf_op jit(solution)/shard_map/ppermute | solution.py:347
  16.3 6.2 %collective-permute-start.4 = (f32[2,8,16,128]{3,2,1,0:T(8,128)S(1)}, f32[2,8,16,128]{3,2,1,0:T(8,128)S(1)}, u32[]{:S(2)}, u32[]{:S(2)}) collective-permute-start(f32[2,8,16,128]{3,2,1,0:T(8,128)S(1)} %get-tuple-element.8), channel_id=1, source_target_pairs={{0,152},{32,184},{64,216},{96,248},{8,0},{40,32},{72,64},{104,96},... | collective-permute-start | bytes 393224 | tf_op jit(solution)/shard_map/ppermute | solution.py:348
  17.5 0.7 copy-start.8
  22.6 7.3 %copy-start.1 = (f32[4,2,8,16,128]{4,3,2,1,0:T(8,128)}, f32[4,2,8,16,128]{4,3,2,1,0:T(8,128)S(1)}, u32[]{:S(2)}) copy-start(f32[4,2,8,16,128]{4,3,2,1,0:T(8,128)S(1)} %pad_maximum_fusion.own) | copy-start | bytes 1572868
  22.6 19.8 %collective-permute-start.7 = (f32[4,2,8,16,128]{4,3,2,1,0:T(8,128)S(1)}, f32[4,2,8,16,128]{4,3,2,1,0:T(8,128)S(1)}, u32[]{:S(2)}, u32[]{:S(2)}) collective-permute-start(f32[4,2,8,16,128]{4,3,2,1,0:T(8,128)S(1)} %pad_maximum_fusion.own), channel_id=1, source_target_pairs={{1,0},{2,1},{3,2},{4,3},{5,4},{6,5},{7,6},{9,8},{10,9},{11,10},{12... | collective-permute-start | bytes 1572872 | tf_op jit(solution)/shard_map/ppermute | solution.py:354
  26.8 15.7 %collective-permute-start.6 = (f32[4,2,8,16,128]{4,3,2,1,0:T(8,128)S(1)}, f32[4,2,8,16,128]{4,3,2,1,0:T(8,128)S(1)}, u32[]{:S(2)}, u32[]{:S(2)}) collective-permute-start(f32[4,2,8,16,128]{4,3,2,1,0:T(8,128)S(1)} %pad_maximum_fusion.own), channel_id=1, source_target_pairs={{0,1},{1,2},{2,3},{3,4},{4,5},{5,6},{6,7},{8,9},{9,10},{10,11},{11... | collective-permute-start | bytes 1572872 | tf_op jit(solution)/shard_map/ppermute | solution.py:354
  29.9 10.2 %collective-permute-start.8 = (f32[4,2,8,8,128]{4,3,2,1,0:T(8,128)S(1)}, f32[4,2,8,8,128]{4,3,2,1,0:T(8,128)S(1)}, u32[]{:S(2)}, u32[]{:S(2)}) collective-permute-start(f32[4,2,8,8,128]{4,3,2,1,0:T(8,128)S(1)} %get-tuple-element.5), channel_id=1, source_target_pairs={{2,0},{3,1},{4,2},{5,3},{6,4},{7,5},{10,8},{11,9},{12,10},{13,11},... | collective-permute-start | bytes 786440 | tf_op jit(solution)/shard_map/ppermute | solution.py:354
  32.0 10.4 %collective-permute-start.5 = (f32[4,2,8,8,128]{4,3,2,1,0:T(8,128)S(1)}, f32[4,2,8,8,128]{4,3,2,1,0:T(8,128)S(1)}, u32[]{:S(2)}, u32[]{:S(2)}) collective-permute-start(f32[4,2,8,8,128]{4,3,2,1,0:T(8,128)S(1)} %get-tuple-element.6), channel_id=1, source_target_pairs={{0,2},{1,3},{2,4},{3,5},{4,6},{5,7},{8,10},{9,11},{10,12},{11,13},... | collective-permute-start | bytes 786440 | tf_op jit(solution)/shard_map/ppermute | solution.py:354
  35.2 0.7 copy-start.7
  40.1 3.1 %copy-start.4 = (f32[4,2,8,8,128]{4,3,2,1,0:T(8,128)}, f32[4,2,8,8,128]{4,3,2,1,0:T(8,128)S(1)}, u32[]{:S(2)}) copy-start(f32[4,2,8,8,128]{4,3,2,1,0:T(8,128)S(1)} %collective-permute-done.8.far_right) | copy-start | bytes 786436
  42.4 0.7 copy-start.5
  42.4 0.9 copy-start.2
  42.4 1.1 copy-start.3
where the time goes:
time: 166 us
  Pallas kernels  122 us (73%)
  starting transfers between devices  29.1 us (18%)
  waiting for transfers between devices  10.5 us (6%)
  local copies, waits for them, and re-layouts  2.28 us (1%)
    pallas_call x1, Pallas kernels, predict(): pl.pallas_call(kernel, out_shape=jax.ShapeDtypeStruct((6, OWN_Y, OWN_Z, L...  122 us
    ppermute x2, starting transfers between devices, lookup_tables(): lax.ppermute(plan, 'tm', [(i, i + back) for i in range(count - back)])  13.4 us
    ppermute x4, starting transfers between devices, shifted(): lax.ppermute(block, 'gz', [(i, i + step) for i in range(count) if 0 <= i...  12.5 us
    ppermute x4, waiting for transfers between devices, shifted(): lax.ppermute(block, 'gz', [(i, i + step) for i in range(count) if 0 <= i...  6.55 us
  transfers between devices with their start and end apart: 9, of which 5 were waited for; matrix products, arithmetic and copies ran while one was open for 1% of the time, Pallas kernels for 0%

commit v1 on v0

v1 whole, which is shorter than its diff:
```python
import functools
import math

import jax
import jax.numpy as jnp
import numpy as np
from jax import lax
from jax.experimental import pallas as pl
from jax.experimental.pallas import tpu as pltpu
from jax.sharding import PartitionSpec as P

STEPS = 8
TERMS = 8
lame_ratio = 2.5
mass_top = 2.0
step_squared = 1.0

PLANES = 32
OWN_Y = 8
OWN_Z = 16
HALO = 24
ROWS = HALO + OWN_Z + HALO
PAD = 8
LANES = 128
CHUNK = 16
UNROLL = 4
BOX = PLANES + 2 * UNROLL + 4
NEAR = TERMS - 1


def cheb_tables():
    spectrum_top = mass_top * 12.0 * (1.0 + lame_ratio)
    time_step = math.sqrt(step_squared / spectrum_top)
    horizon = STEPS * time_step
    angles = np.pi * (np.arange(TERMS) + 0.5) / TERMS
    node_x = 0.5 * spectrum_top * (1.0 + np.cos(angles))
    node_root = np.sqrt(node_x)
    values_c = np.cos(horizon * node_root)
    values_s = np.sin(horizon * node_root) / node_root
    values_g = node_root * np.sin(horizon * node_root)

    def project_values(values):
        result = np.array([2.0 / TERMS * np.sum(values * np.cos(k * angles)) for k in range(TERMS)])
        result[0] = 0.5 * result[0]
        return [float(entry) for entry in result]

    return (
        spectrum_top,
        time_step,
        project_values(values_c),
        project_values(values_s),
        project_values(values_g),
    )


def columns(reach):
    return (HALO - reach) // 8, -(-(HALO + OWN_Z + reach) // 8)


def span(reach):
    count = min(8, reach) + OWN_Y + min(16, reach)
    return count + -count % UNROLL


def along_x():
    near = np.eye(LANES, k=1) + np.eye(LANES, k=-1) - 6.0 * np.eye(LANES)
    near_x = near.copy()
    near_x[0, 0] -= lame_ratio
    step = lame_ratio * (np.eye(LANES, k=-1) - np.eye(LANES))
    pair = np.concatenate([near_x, step], axis=1)
    near = np.concatenate([near, 0.0 * near], axis=1)
    return [jnp.asarray(np.concatenate([m, m]), jnp.bfloat16) for m in (near, pair)]


def lookup(table, index):
    numbers = lax.GatherDimensionNumbers(
        offset_dims=(), collapsed_slice_dims=(1,), start_index_map=(1,),
        operand_batching_dims=(0,), start_indices_batching_dims=(0,),
    )
    return lax.gather(
        table, index[..., None], numbers, (1, 1), mode=lax.GatherScatterMode.PROMISE_IN_BOUNDS
    )


def kernel(
    place_ref, near_ref, pair_ref, table_ref, far_left, left, own, right, far_right, out_ref,
    mass, mass4, actor, dirs, disp, vel, spare_u, spare_v, total, div_u, div_v,
):
    accs = [pltpu.ACC(0 if c < 2 else 1)((CHUNK, 2 * LANES), jnp.float32) for _ in range(2) for c in range(3) for _ in range(UNROLL) for _ in range(ROWS // CHUNK)]

    def scope(*held):
        pltpu.matmul_push_rhs(near_ref[...], 0, 0)
        pltpu.matmul_push_rhs(pair_ref[...], 0, 1)
        work(
            held, place_ref, table_ref, far_left, left, own, right, far_right, out_ref,
            mass, mass4, actor, dirs, disp, vel, spare_u, spare_v, total, div_u, div_v,
        )

    pl.run_scoped(scope, *accs)


def work(
    held, place_ref, table_ref, far_left, left, own, right, far_right, out_ref,
    mass, mass4, actor, dirs, disp, vel, spare_u, spare_v, total, div_u, div_v,
):
    spectrum_top, time_step, coef_c, coef_s, coef_g = cheb_tables()
    here = place_ref[0]
    home = here * OWN_Y
    fresh = [True, True]

    def acc_of(which, c, q, pair):
        return held[((which * 3 + c) * UNROLL + q) * (ROWS // CHUNK) + pair]

    def lane_of(value):
        return lax.broadcasted_iota(jnp.int32, value.shape, 1)

    def after(value):
        return jnp.where(lane_of(value) != LANES - 1, pltpu.roll(value, LANES - 1, 1), 0.0)

    def before(value):
        return jnp.where(lane_of(value) != 0, pltpu.roll(value, 1, 1), 0.0)

    def rows_of(column):
        return PAD + column * 8

    def lowest(reach):
        return jnp.clip(home - reach, 0, PLANES - span(reach)) + 1

    edge = jnp.zeros((PAD + ROWS + PAD, LANES), jnp.float32)
    for ref in (disp, vel, spare_u, spare_v):
        for c in range(3):
            for plane in [0] + list(range(PLANES + 1, BOX)):
                ref[c, plane, :, :] = edge

    for slot in range(4):
        first = lax.rem(here + 4 - slot, 4) * OWN_Y + 1

        @pl.loop(0, OWN_Y)
        def _(y):
            plane = first + y
            row = 0
            for piece in (far_left, left, own, right, far_right):
                for part in range(0, piece.shape[-2], 8):
                    at = pl.ds(PAD + row, 8)
                    weight = piece[slot, 0, y, part : part + 8, :] * (1.0 / spectrum_top)
                    index = piece[slot, 1, y, part : part + 8, :].astype(jnp.int32)
                    mass[plane, at, :] = weight
                    mass4[plane, at, :] = -4.0 * weight
                    actor[plane, at, :] = index
                    for c in range(3):
                        dirs[c, plane, at, :] = lookup(table_ref[27 + c, :8], index)
                    row += 8

    def divergence(field, plane, low):
        at = pl.ds(low, 8)
        u0, u1, u2 = (field[c, plane, at, :] for c in range(3))
        value = (field[0, plane + 1, at, :] - u0) + (field[1, plane, pl.ds(low + 1, 8), :] - u1)
        return (value + (after(u2) - u2)) * lame_ratio

    def spread(which, field, planes, cols):
        for pair, low in enumerate(range(rows_of(cols[0]), rows_of(cols[1]), CHUNK)):
            for q, plane in enumerate(planes):
                for c in range(3):
                    value = field[c, plane, pl.ds(low, CHUNK), :]
                    high = value.astype(jnp.bfloat16)
                    rest = (value - high.astype(jnp.float32)).astype(jnp.bfloat16)
                    unit = 0 if c < 2 else 1
                    pltpu.matmul_acc_lhs(
                        acc_of(which, c, q, pair),
                        jnp.concatenate([high, rest], axis=1),
                        load_staged_rhs=0 if fresh[unit] else None,
                    )
                    fresh[unit] = False

    def combine(which, field, div, planes, low, pair):
        at = pl.ds(low, CHUNK)
        around = [planes[0] - 1] + planes + [planes[-1] + 1]
        u = [[field[c, p, at, :] for p in around] for c in range(3)]
        p_before = div[around[0], at, :]
        found = []
        for q, plane in enumerate(planes):
            ahead = [field[c, plane, pl.ds(low + 1, CHUNK), :] for c in range(3)]
            behind = [field[c, plane, pl.ds(low - 1, CHUNK), :] for c in range(3)]
            centre = [u[c][q + 1] for c in range(3)]
            flat = [pltpu.matmul_pop(acc_of(which, c, q, pair)) for c in range(3)]
            step = flat[2][:, LANES:]
            p = ((u[0][q + 2] - centre[0]) + (ahead[1] - centre[1])) * lame_ratio + step
            div[plane, at, :] = p
            sums = [
                ((u[c][q] + u[c][q + 2]) + (ahead[c] + behind[c])) + (flat[c][:, :LANES] + p)
                for c in range(3)
            ]
            sums[0] = sums[0] - p_before
            sums[1] = sums[1] - div[plane, pl.ds(low - 1, CHUNK), :]
            sums[2] = sums[2] - before(p)
            p_before = p
            found.append((centre, sums))
        return found

    def sweep(reach, fields, head, each):
        j0, j1 = columns(reach)
        j0p = j0 - 1 if (HALO - reach) % 8 == 0 else j0
        begin = lowest(reach)

        def edges(plane, cols):
            for low in range(rows_of(cols[0]), rows_of(cols[1]), 8):
                for field, div in fields:
                    div[plane, pl.ds(low, 8), :] = divergence(field, plane, low)

        def prepare(first):
            for which, (field, div) in enumerate(fields):
                spread(which, field, [first + q for q in range(UNROLL)], (j0, j1))

        if head is not None:
            @pl.loop(0, 2 * UNROLL + 2)
            def _(i):
                head(begin - 1 + i)
        edges(begin - 1, (j0, j1))
        prepare(begin)

        @pl.loop(0, span(reach) // UNROLL)
        def _(trip):
            first = begin + trip * UNROLL
            planes = [first + q for q in range(UNROLL)]
            if j0p < j0:
                for plane in planes:
                    edges(plane, (j0p, j0))
            for pair, low in enumerate(range(rows_of(j0), rows_of(j1), CHUNK)):
                each(planes, low, pair)
            prepare(first + UNROLL)
            if head is not None:
                for q in range(UNROLL):
                    head(first + 2 * UNROLL + 1 + q)

        for which in range(len(fields)):
            for c in range(3):
                for q in range(UNROLL):
                    for pair in range((j1 - j0) // 2):
                        pltpu.matmul_pop(acc_of(which, c, q, pair))

    def drive(window, reach_last):
        def amplitude(n, plane, at):
            return lookup(table_ref[window * 9 + n], actor[plane, at, :])

        reach = reach_last + STEPS
        j0, j1 = columns(reach)

        @pl.loop(0, span(reach))
        def _(y):
            plane = lowest(reach) + y
            for low in range(rows_of(j0), rows_of(j1), CHUNK):
                at = pl.ds(low, CHUNK)
                push = (0.5 * mass[plane, at, :]) * amplitude(0, plane, at)
                for c in range(3):
                    moved = push * dirs[c, plane, at, :]
                    disp[c, plane, at, :] = moved
                    vel[c, plane, at, :] = moved

        for n in range(STEPS):
            reach = reach_last + STEPS - 1 - n
            j0, j1 = columns(reach + 1)
            last = n == STEPS - 1

            def head(plane):
                for low in range(rows_of(j0), rows_of(j1), CHUNK):
                    at = pl.ds(low, CHUNK)
                    for c in range(3):
                        disp[c, plane, at, :] = disp[c, plane, at, :] + vel[c, plane, at, :]

            def each(planes, low, pair):
                at = pl.ds(low, CHUNK)
                for plane, (centre, sums) in zip(planes, combine(0, disp, div_u, planes, low, pair)):
                    amp = amplitude(n + 1, plane, at)
                    weight = mass[plane, at, :]
                    for c in range(3):
                        change = weight * (dirs[c, plane, at, :] * amp + sums[c])
                        if last:
                            ended = vel[c, plane, at, :] + 0.5 * change
                            vel[c, plane, at, :] = ended * (1.0 / time_step)
                        else:
                            vel[c, plane, at, :] = vel[c, plane, at, :] + change

            sweep(reach, [(disp, div_u)], head if n else None, each)

    def propagate(reach_last):
        even, odd = (disp, vel), (spare_u, spare_v)
        divs = (div_u, div_v)
        j0, j1 = columns(reach_last)
        begin = lowest(reach_last)

        def gather(k):
            @pl.loop(0, span(reach_last))
            def _(y):
                plane = begin + y
                for low in range(rows_of(j0), rows_of(j1), CHUNK):
                    at = pl.ds(low, CHUNK)
                    to = pl.ds(low - rows_of(j0), CHUNK)
                    for c in range(3):
                        u0, v0 = (ref[c, plane, at, :] for ref in even)
                        u1, v1 = (ref[c, plane, at, :] for ref in odd)
                        new_u = (coef_c[k] * u0 + coef_s[k] * v0) + (
                            coef_c[k + 1] * u1 + coef_s[k + 1] * v1
                        )
                        new_v = (coef_c[k] * v0 - coef_g[k] * u0) + (
                            coef_c[k + 1] * v1 - coef_g[k + 1] * u1
                        )
                        if k:
                            new_u = total[c, y, to, :] + new_u
                            new_v = total[3 + c, y, to, :] + new_v
                        total[c, y, to, :] = new_u
                        total[3 + c, y, to, :] = new_v

        for k in range(1, TERMS):
            reach = reach_last + TERMS - 1 - k
            source, target = (even, odd) if k % 2 else (odd, even)

            def each(planes, low, pair):
                at = pl.ds(low, CHUNK)
                for which, (field, div, result) in enumerate(zip(source, divs, target)):
                    found = combine(which, field, div, planes, low, pair)
                    for plane, (centre, sums) in zip(planes, found):
                        weight = mass4[plane, at, :]
                        for c in range(3):
                            if k == 1:
                                value = (0.5 * weight) * sums[c] - centre[c]
                            else:
                                old = result[c, plane, at, :]
                                value = weight * sums[c] - ((centre[c] + centre[c]) + old)
                            result[c, plane, at, :] = value

            sweep(reach, list(zip(source, divs)), None, each)
            if k % 2:
                gather(k - 1)

    drive(0, 2 * (TERMS - 1))
    propagate(TERMS - 1)
    drive(1, TERMS - 1)
    j0, j1 = columns(TERMS - 1)

    @pl.loop(0, span(TERMS - 1))
    def _(y):
        plane = lowest(TERMS - 1) + y
        for low in range(rows_of(j0), rows_of(j1), CHUNK):
            at = pl.ds(low, CHUNK)
            to = pl.ds(low - rows_of(j0), CHUNK)
            for c in range(3):
                disp[c, plane, at, :] = disp[c, plane, at, :] + total[c, y, to, :]
                vel[c, plane, at, :] = vel[c, plane, at, :] + total[3 + c, y, to, :]

    propagate(0)
    drive(2, 0)

    @pl.loop(0, OWN_Y)
    def _(y):
        plane = home + 1 + y
        at = pl.ds(PAD + HALO, OWN_Z)
        for c in range(3):
            out_ref[c, y, :, :] = disp[c, plane, at, :] + total[c, y, :OWN_Z, :]
            out_ref[3 + c, y, :, :] = vel[c, plane, at, :] + total[3 + c, y, :OWN_Z, :]


def predict(place, table, far_left, left, own, right, far_right):
    box = (BOX, PAD + ROWS + PAD, LANES)
    f32 = jnp.float32
    vmem = pl.BlockSpec(memory_space=pltpu.VMEM)
    j0, j1 = columns(NEAR)
    return pl.pallas_call(
        kernel,
        out_shape=jax.ShapeDtypeStruct((6, OWN_Y, OWN_Z, LANES), f32),
        in_specs=[pl.BlockSpec(memory_space=pltpu.SMEM)] + [vmem] * 8,
        out_specs=vmem,
        scratch_shapes=[pltpu.VMEM(box, f32)] * 2
        + [pltpu.VMEM(box, jnp.int32), pltpu.VMEM((3,) + box, f32)]
        + [pltpu.VMEM((3,) + box, f32)] * 4
        + [pltpu.VMEM((6, span(NEAR), 8 * (j1 - j0), LANES), f32)]
        + [pltpu.VMEM(box, f32)] * 2,
        compiler_params=pltpu.CompilerParams(vmem_limit_bytes=60 * 1024 * 1024),
    )(place, *along_x(), table, far_left, left, own, right, far_right)


def lookup_tables(plan, profiles, directions):
    window = lax.axis_index("tm")
    count = lax.axis_size("tm")
    plans = [
        lax.ppermute(plan, "tm", [(i, i + back) for i in range(count - back)]) for back in (2, 1)
    ] + [plan]
    rows = []
    for back, ids in zip((2, 1, 0), plans):
        picked = ids[0][:, None] == jnp.arange(profiles.shape[0], dtype=jnp.int32)[None, :]
        picked = jnp.where(window >= back, picked, False).astype(jnp.float32)
        chosen = jnp.dot(
            picked, profiles, precision=lax.Precision.HIGHEST, preferred_element_type=jnp.float32
        )
        rows.append(chosen.T)
    table = jnp.concatenate(rows + [directions], axis=0)
    table = jnp.pad(table, ((0, 2), (0, LANES - table.shape[1])))
    return jnp.broadcast_to(table[:, None, :], (32, CHUNK, LANES))


def ring_steps(step):
    pairs = []
    for ring in range(8):
        move = step(ring)
        goal = (ring + move) % 8
        for y in range(4):
            source = ((ring // 4) * 4 + y) * 4 + ring % 4
            target = ((goal // 4) * 4 + y) * 4 + goal % 4
            pairs.append((source, target))
    return pairs


def body(inverse_mass, actuator_of_cell, plan_ids, profiles, directions):
    place = lax.axis_index("gy").astype(jnp.int32)[None]
    packed = jnp.stack([inverse_mass, actuator_of_cell.astype(jnp.float32)])
    table = lookup_tables(plan_ids, profiles, directions)
    from_lower = lax.ppermute(packed, ("tm", "gy"), ring_steps(lambda ring: 1))
    from_upper = lax.ppermute(packed, ("tm", "gy"), ring_steps(lambda ring: 7))
    opposite = lax.ppermute(packed, ("tm", "gy"), ring_steps(lambda ring: 2 if ring % 2 else 6))
    column = jnp.stack([packed, from_lower, opposite, from_upper])
    count = lax.axis_size("gz")

    def shifted(block, step):
        return lax.ppermute(
            block, "gz", [(i, i + step) for i in range(count) if 0 <= i + step < count]
        )

    left = shifted(column, 1)
    right = shifted(column, -1)
    far_left = shifted(column[..., 8:, :], 2)
    far_right = shifted(column[..., :8, :], -2)
    result = predict(place, table, far_left, left, column, right, far_right)
    return result[None]


def solution(mesh):
    in_specs = (P("gy", "gz", None), P("gy", "gz", None), P("tm", None), P(), P())
    out_specs = P("tm", None, "gy", "gz", None)
    return jax.shard_map(body, mesh=mesh, in_specs=in_specs, out_specs=out_specs, check_vma=False)
```

time: 166 us -> 136 us (0.82)
  Pallas kernels: 122 us -> 92.3 us
    pallas_call x1, Pallas kernels: 122 us -> 92.3 us  [predict(): pl.pallas_call(kernel, out_shape=jax.ShapeDtypeStruct((6, OWN_Y, OWN_Z, L...]
where the time goes in v1:
time: 136 us
  Pallas kernels  92.3 us (68%)
  starting transfers between devices  29.1 us (21%)
  waiting for transfers between devices  10.5 us (8%)
  local copies, waits for them, and re-layouts  2.34 us (2%)
    pallas_call x1, Pallas kernels, predict(): pl.pallas_call(kernel, out_shape=jax.ShapeDtypeStruct((6, OWN_Y, OWN_Z, L...  92.3 us
    ppermute x2, starting transfers between devices, lookup_tables(): lax.ppermute(plan, 'tm', [(i, i + back) for i in range(count - back)])  13.4 us
    ppermute x4, starting transfers between devices, shifted(): lax.ppermute(block, 'gz', [(i, i + step) for i in range(count) if 0 <= i...  12.5 us
    ppermute x4, waiting for transfers between devices, shifted(): lax.ppermute(block, 'gz', [(i, i + step) for i in range(count) if 0 <= i...  6.55 us
    ppermute x1, waiting for transfers between devices, body(): from_lower = lax.ppermute(packed, ('tm', 'gy'), ring_steps(lambda ring: 1))  3.24 us
  transfers between devices with their start and end apart: 9, of which 5 were waited for; matrix products, arithmetic and copies ran while one was open for 1% of the time, Pallas kernels for 0%

profile of v1, /device:TPU:27, one launch (start us, length us, event | category | flops | bytes accessed | tf_op | source)
XLA Modules:
  0.0 135.9 jit_solution(10326227478515504138)
XLA Ops:
  0.0 0.0 copy-start
  0.0 0.0 copy-start.6
  0.0 9.6 %collective-permute-start = (s32[1,32]{1,0:T(1,128)}, s32[1,32]{1,0:T(1,128)S(1)}, u32[]{:S(2)}, u32[]{:S(2)}) collective-permute-start(s32[1,32]{1,0:T(1,128)} %param.9), channel_id=1, source_target_pairs={{0,64},{32,96},{64,128},{96,160},{128,192},{160,224},{1,65},{33,97... | collective-permute-start | bytes 392 | tf_op jit(solution)/shard_map/ppermute | solution.py:385
  9.6 3.8 %collective-permute-start.1 = (s32[1,32]{1,0:T(1,128)}, s32[1,32]{1,0:T(1,128)S(1)}, u32[]{:S(2)}, u32[]{:S(2)}) collective-permute-start(s32[1,32]{1,0:T(1,128)} %param.9), channel_id=1, source_target_pairs={{0,32},{32,64},{64,96},{96,128},{128,160},{160,192},{192,224},{1,3... | collective-permute-start | bytes 392 | tf_op jit(solution)/shard_map/ppermute | solution.py:385
  13.4 0.8 convert_bitcast_fusion
  14.3 0.0 copy-done.6
  14.3 0.1 collective-permute-start.3
  14.4 1.9 %collective-permute-start.2 = (f32[2,8,16,128]{3,2,1,0:T(8,128)S(1)}, f32[2,8,16,128]{3,2,1,0:T(8,128)S(1)}, u32[]{:S(2)}, u32[]{:S(2)}) collective-permute-start(f32[2,8,16,128]{3,2,1,0:T(8,128)S(1)} %get-tuple-element.8), channel_id=1, source_target_pairs={{0,8},{32,40},{64,72},{96,104},{8,16},{40,48},{72,80},{104,112},{1... | collective-permute-start | bytes 393224 | tf_op jit(solution)/shard_map/ppermute | solution.py:416
  16.3 1.2 collective-permute-start.4
  17.5 0.0 copy-start.8
  17.5 0.0 copy-done
  17.5 0.7 copy-done.8
  18.2 0.2 convolution_bitcast_fusion
  18.4 0.0 collective-permute-done
  18.4 0.2 convolution_bitcast_fusion.2
  18.6 0.5 collective-permute-done.3
  19.1 3.2 %collective-permute-done.2 = f32[2,8,16,128]{3,2,1,0:T(8,128)S(1)} collective-permute-done((f32[2,8,16,128]{3,2,1,0:T(8,128)S(1)}, f32[2,8,16,128]{3,2,1,0:T(8,128)S(1)}, u32[]{:S(2)}, u32[]{:S(2)}) %collective-permute-start.2) | collective-permute-done | bytes 131104 | tf_op jit(solution)/shard_map/ppermute | solution.py:416
  22.4 0.1 collective-permute-done.4
  22.6 0.0 copy-start.1
  22.6 4.2 %collective-permute-start.7 = (f32[4,2,8,16,128]{4,3,2,1,0:T(8,128)S(1)}, f32[4,2,8,16,128]{4,3,2,1,0:T(8,128)S(1)}, u32[]{:S(2)}, u32[]{:S(2)}) collective-permute-start(f32[4,2,8,16,128]{4,3,2,1,0:T(8,128)S(1)} %pad_maximum_fusion.own), channel_id=1, source_target_pairs={{1,0},{2,1},{3,2},{4,3},{5,4},{6,5},{7,6},{9,8},{10,9},{11,10},{12... | collective-permute-start | bytes 1572872 | tf_op jit(solution)/shard_map/ppermute | solution.py:423
  26.8 3.0 %collective-permute-start.6 = (f32[4,2,8,16,128]{4,3,2,1,0:T(8,128)S(1)}, f32[4,2,8,16,128]{4,3,2,1,0:T(8,128)S(1)}, u32[]{:S(2)}, u32[]{:S(2)}) collective-permute-start(f32[4,2,8,16,128]{4,3,2,1,0:T(8,128)S(1)} %pad_maximum_fusion.own), channel_id=1, source_target_pairs={{0,1},{1,2},{2,3},{3,4},{4,5},{5,6},{6,7},{8,9},{9,10},{10,11},{11... | collective-permute-start | bytes 1572872 | tf_op jit(solution)/shard_map/ppermute | solution.py:423
  29.8 0.1 fusion.19
  29.8 0.0 copy-done.1
  29.9 2.2 %collective-permute-start.8 = (f32[4,2,8,8,128]{4,3,2,1,0:T(8,128)S(1)}, f32[4,2,8,8,128]{4,3,2,1,0:T(8,128)S(1)}, u32[]{:S(2)}, u32[]{:S(2)}) collective-permute-start(f32[4,2,8,8,128]{4,3,2,1,0:T(8,128)S(1)} %get-tuple-element.5), channel_id=1, source_target_pairs={{2,0},{3,1},{4,2},{5,3},{6,4},{7,5},{10,8},{11,9},{12,10},{13,11},... | collective-permute-start | bytes 786440 | tf_op jit(solution)/shard_map/ppermute | solution.py:423
  32.0 3.1 %collective-permute-start.5 = (f32[4,2,8,8,128]{4,3,2,1,0:T(8,128)S(1)}, f32[4,2,8,8,128]{4,3,2,1,0:T(8,128)S(1)}, u32[]{:S(2)}, u32[]{:S(2)}) collective-permute-start(f32[4,2,8,8,128]{4,3,2,1,0:T(8,128)S(1)} %get-tuple-element.6), channel_id=1, source_target_pairs={{0,2},{1,3},{2,4},{3,5},{4,6},{5,7},{8,10},{9,11},{10,12},{11,13},... | collective-permute-start | bytes 786440 | tf_op jit(solution)/shard_map/ppermute | solution.py:423
  35.2 0.0 collective-permute-done.1
  35.2 0.0 copy-start.7
  35.2 0.2 convolution_bitcast_fusion.1
  35.4 0.5 copy-done.7
  35.9 4.2 %collective-permute-done.8.far_right = f32[4,2,8,8,128]{4,3,2,1,0:T(8,128)S(1)} collective-permute-done((f32[4,2,8,8,128]{4,3,2,1,0:T(8,128)S(1)}, f32[4,2,8,8,128]{4,3,2,1,0:T(8,128)S(1)}, u32[]{:S(2)}, u32[]{:S(2)}) %collective-permute-start.8) | collective-permute-done | bytes 262176 | tf_op jit(solution)/shard_map/ppermute | solution.py:423
  40.1 0.0 copy-start.4
  40.1 2.3 %collective-permute-done.5.far_left = f32[4,2,8,8,128]{4,3,2,1,0:T(8,128)S(1)} collective-permute-done((f32[4,2,8,8,128]{4,3,2,1,0:T(8,128)S(1)}, f32[4,2,8,8,128]{4,3,2,1,0:T(8,128)S(1)}, u32[]{:S(2)}, u32[]{:S(2)}) %collective-permute-start.5) | collective-permute-done | bytes 262176 | tf_op jit(solution)/shard_map/ppermute | solution.py:423
  42.4 0.0 copy-start.5
  42.4 0.0 collective-permute-done.7.right
  42.4 0.0 copy-start.2
  42.4 0.0 collective-permute-done.6.left
  42.4 0.0 copy-start.3
  42.4 0.8 broadcast_in_dim.23.table_ref
  43.2 0.0 copy-done.4
  43.2 0.0 copy-done.5
  43.2 0.2 copy-done.2
  43.4 0.2 copy-done.3
  43.6 92.3 %shard_map.73 = f32[6,8,16,128]{3,2,1,0:T(8,128)} custom-call(s32[1]{0:T(128)} %bitcast.place_ref, bf16[256,256]{1,0:T(8,128)(2,1)} %constant.24.clone.near_ref, bf16[256,256]{1,0:T(8,128)(2,1)} %constant.25.clone.pair_ref, f32[32,16,128]{2,1,0:T(8,128)} %broadcast_in_dim.23.table_ref, f32[4,2,8,8,128]{4,3,2,1,0:T(8,128)} %copy-done.5, ...), custom_call_target="tpu_custom_call" | custom-call | tf_op jit(solution)/shard_map/pallas_call | solution.py:367
  (3 shorter events, 0.1 us)
Async XLA Ops:
  0.0 17.5 %copy-start = (f32[16,9]{1,0:T(8,128)S(1)}, f32[16,9]{1,0:T(8,128)}, u32[]{:S(2)}) copy-start(f32[16,9]{1,0:T(8,128)} %param.10) | copy-start | bytes 1732
  0.0 14.3 %copy-start.6 = (f32[8,16,128]{2,1,0:T(8,128)S(1)}, f32[8,16,128]{2,1,0:T(8,128)}, u32[]{:S(2)}) copy-start(f32[8,16,128]{2,1,0:T(8,128)} %param.7) | copy-start | bytes 196612
  0.0 18.4 %collective-permute-start = (s32[1,32]{1,0:T(1,128)}, s32[1,32]{1,0:T(1,128)S(1)}, u32[]{:S(2)}, u32[]{:S(2)}) collective-permute-start(s32[1,32]{1,0:T(1,128)} %param.9), channel_id=1, source_target_pairs={{0,64},{32,96},{64,128},{96,160},{128,192},{160,224},{1,65},{33,97... | collective-permute-start | bytes 392 | tf_op jit(solution)/shard_map/ppermute | solution.py:385
  9.6 25.5 %collective-permute-start.1 = (s32[1,32]{1,0:T(1,128)}, s32[1,32]{1,0:T(1,128)S(1)}, u32[]{:S(2)}, u32[]{:S(2)}) collective-permute-start(s32[1,32]{1,0:T(1,128)} %param.9), channel_id=1, source_target_pairs={{0,32},{32,64},{64,96},{96,128},{128,160},{160,192},{192,224},{1,3... | collective-permute-start | bytes 392 | tf_op jit(solution)/shard_map/ppermute | solution.py:385
  14.3 4.8 %collective-permute-start.3 = (f32[2,8,16,128]{3,2,1,0:T(8,128)S(1)}, f32[2,8,16,128]{3,2,1,0:T(8,128)S(1)}, u32[]{:S(2)}, u32[]{:S(2)}) collective-permute-start(f32[2,8,16,128]{3,2,1,0:T(8,128)S(1)} %get-tuple-element.8), channel_id=1, source_target_pairs={{0,144},{32,176},{64,208},{96,240},{8,24},{40,56},{72,88},{104,120... | collective-permute-start | bytes 393224 | tf_op jit(solution)/shard_map/ppermute | solution.py:418
  14.4 8.0 %collective-permute-start.2 = (f32[2,8,16,128]{3,2,1,0:T(8,128)S(1)}, f32[2,8,16,128]{3,2,1,0:T(8,128)S(1)}, u32[]{:S(2)}, u32[]{:S(2)}) collective-permute-start(f32[2,8,16,128]{3,2,1,0:T(8,128)S(1)} %get-tuple-element.8), channel_id=1, source_target_pairs={{0,8},{32,40},{64,72},{96,104},{8,16},{40,48},{72,80},{104,112},{1... | collective-permute-start | bytes 393224 | tf_op jit(solution)/shard_map/ppermute | solution.py:416
  16.3 6.2 %collective-permute-start.4 = (f32[2,8,16,128]{3,2,1,0:T(8,128)S(1)}, f32[2,8,16,128]{3,2,1,0:T(8,128)S(1)}, u32[]{:S(2)}, u32[]{:S(2)}) collective-permute-start(f32[2,8,16,128]{3,2,1,0:T(8,128)S(1)} %get-tuple-element.8), channel_id=1, source_target_pairs={{0,152},{32,184},{64,216},{96,248},{8,0},{40,32},{72,64},{104,96},... | collective-permute-start | bytes 393224 | tf_op jit(solution)/shard_map/ppermute | solution.py:417
  17.5 0.7 copy-start.8
  22.6 7.3 %copy-start.1 = (f32[4,2,8,16,128]{4,3,2,1,0:T(8,128)}, f32[4,2,8,16,128]{4,3,2,1,0:T(8,128)S(1)}, u32[]{:S(2)}) copy-start(f32[4,2,8,16,128]{4,3,2,1,0:T(8,128)S(1)} %pad_maximum_fusion.own) | copy-start | bytes 1572868
  22.6 19.8 %collective-permute-start.7 = (f32[4,2,8,16,128]{4,3,2,1,0:T(8,128)S(1)}, f32[4,2,8,16,128]{4,3,2,1,0:T(8,128)S(1)}, u32[]{:S(2)}, u32[]{:S(2)}) collective-permute-start(f32[4,2,8,16,128]{4,3,2,1,0:T(8,128)S(1)} %pad_maximum_fusion.own), channel_id=1, source_target_pairs={{1,0},{2,1},{3,2},{4,3},{5,4},{6,5},{7,6},{9,8},{10,9},{11,10},{12... | collective-permute-start | bytes 1572872 | tf_op jit(solution)/shard_map/ppermute | solution.py:423
  26.8 15.7 %collective-permute-start.6 = (f32[4,2,8,16,128]{4,3,2,1,0:T(8,128)S(1)}, f32[4,2,8,16,128]{4,3,2,1,0:T(8,128)S(1)}, u32[]{:S(2)}, u32[]{:S(2)}) collective-permute-start(f32[4,2,8,16,128]{4,3,2,1,0:T(8,128)S(1)} %pad_maximum_fusion.own), channel_id=1, source_target_pairs={{0,1},{1,2},{2,3},{3,4},{4,5},{5,6},{6,7},{8,9},{9,10},{10,11},{11... | collective-permute-start | bytes 1572872 | tf_op jit(solution)/shard_map/ppermute | solution.py:423
  29.9 10.2 %collective-permute-start.8 = (f32[4,2,8,8,128]{4,3,2,1,0:T(8,128)S(1)}, f32[4,2,8,8,128]{4,3,2,1,0:T(8,128)S(1)}, u32[]{:S(2)}, u32[]{:S(2)}) collective-permute-start(f32[4,2,8,8,128]{4,3,2,1,0:T(8,128)S(1)} %get-tuple-element.5), channel_id=1, source_target_pairs={{2,0},{3,1},{4,2},{5,3},{6,4},{7,5},{10,8},{11,9},{12,10},{13,11},... | collective-permute-start | bytes 786440 | tf_op jit(solution)/shard_map/ppermute | solution.py:423
  32.0 10.4 %collective-permute-start.5 = (f32[4,2,8,8,128]{4,3,2,1,0:T(8,128)S(1)}, f32[4,2,8,8,128]{4,3,2,1,0:T(8,128)S(1)}, u32[]{:S(2)}, u32[]{:S(2)}) collective-permute-start(f32[4,2,8,8,128]{4,3,2,1,0:T(8,128)S(1)} %get-tuple-element.6), channel_id=1, source_target_pairs={{0,2},{1,3},{2,4},{3,5},{4,6},{5,7},{8,10},{9,11},{10,12},{11,13},... | collective-permute-start | bytes 786440 | tf_op jit(solution)/shard_map/ppermute | solution.py:423
  35.2 0.7 copy-start.7
  40.1 3.2 %copy-start.4 = (f32[4,2,8,8,128]{4,3,2,1,0:T(8,128)}, f32[4,2,8,8,128]{4,3,2,1,0:T(8,128)S(1)}, u32[]{:S(2)}) copy-start(f32[4,2,8,8,128]{4,3,2,1,0:T(8,128)S(1)} %collective-permute-done.8.far_right) | copy-start | bytes 786436
  42.4 0.8 copy-start.5
  42.4 1.0 copy-start.2
  42.4 1.2 copy-start.3
